TPU v7x, 32 devices: a whole 2x2x4 slice. The times are simulated.
32 devices in a mesh: pp: 4 (over y, core), cp: 4 (over z), tp: 2 (over x).
Axes of the slice: x: 2, y: 2, z: 4, core: 2. Of those that a mesh axis runs over, the one named last changes fastest.
Arguments:
- queries: bfloat16 [4, 1024, 8192], P('pp', 'cp', 'tp'), may hold values from -150 to 150
- keys: bfloat16 [4, 1024, 1024], P('pp', 'cp', 'tp'), may hold values from -6 to 6
- values: bfloat16 [4, 1024, 1024], P('pp', 'cp', 'tp'), may hold values from -6 to 6
- span_order: int32 [8], replicated, may hold values from 0 to 7, each once
Outputs:
- forwarded: bfloat16 [4, 1024, 8192], P('pp', ('cp', 'tp'))
All inputs are finite; a program needn't handle non-finite values.
Results may differ from a plain program's by a relative error of at most 0.005.
Values may be sent and summed in bfloat16 or wider, within the bound.
A program may use at most 64 MiB of HBM per device.

v0:
```python
import math

import jax
import jax.numpy as jnp
from jax import lax
from jax.sharding import PartitionSpec as P

HD = 128
SPAN = 128


def passed_along(value, axis, steps):
    count = lax.axis_size(axis)
    pairs = [(source, (source + steps) % count) for source in range(count)]
    return lax.ppermute(value, axis, pairs)


def row_positions(span_order, start, count, span):
    rows = start + jnp.arange(count, dtype=jnp.int32)
    which = rows // span
    table = jnp.arange(span_order.shape[0], dtype=jnp.int32)
    picked = jnp.sum(jnp.where(which[:, None] == table[None, :], span_order[None, :], 0), axis=1)
    return picked * span + rows % span


def attend_block(carry, grouped, key_rows, value_rows, query_pos, key_pos):
    running, total, summed = carry
    score = jnp.einsum("qngd,knd->ngqk", grouped, key_rows, preferred_element_type=jnp.float32)
    score = score * (1.0 / HD**0.5)
    visible = (key_pos[None, :] <= query_pos[:, None])[None, None]
    score = jnp.where(visible, score, jnp.float32(-1e30))
    renewed = jnp.maximum(running, jnp.max(score, axis=-1))
    weight = jnp.where(visible, jnp.exp(score - renewed[..., None]), jnp.float32(0.0))
    fade = jnp.exp(running - renewed)
    total = total * fade + jnp.sum(weight, axis=-1)
    mixed = jnp.einsum(
        "ngqk,knd->ngqd",
        weight.astype(jnp.bfloat16),
        value_rows,
        preferred_element_type=jnp.float32,
    )
    summed = summed * fade[..., None] + mixed
    return (renewed, total, summed)


def attend_rows(carry, grouped, key_part, value_part, start, query_pos, span_order, span):
    count_rows = key_part.shape[0]
    kv_heads = grouped.shape[1]
    step_rows = math.gcd(count_rows, span)

    def one_block(index, state):
        first = index * step_rows
        key_rows = lax.dynamic_slice_in_dim(key_part, first, step_rows, 0).reshape(
            step_rows, kv_heads, HD
        )
        value_rows = lax.dynamic_slice_in_dim(value_part, first, step_rows, 0).reshape(
            step_rows, kv_heads, HD
        )
        key_pos = row_positions(span_order, start + first, step_rows, span)
        return attend_block(state, grouped, key_rows, value_rows, query_pos, key_pos)

    return lax.fori_loop(0, count_rows // step_rows, one_block, carry)


def to_tokens(attended):
    return lax.all_to_all(attended, "tp", split_axis=0, concat_axis=1, tiled=True)


def to_next(attended):
    return passed_along(attended, "pp", 1)


def shards(queries, keys, values, span_order):
    query_rows = queries[0]
    key_local = keys[0]
    value_local = values[0]
    local_rows = query_rows.shape[0]
    span = SPAN
    kv_heads = key_local.shape[1] // HD
    group = query_rows.shape[1] // HD // kv_heads
    my_rank = lax.axis_index("cp")
    ranks = lax.axis_size("cp")
    grouped = query_rows.reshape(local_rows, kv_heads, group, HD)
    query_pos = row_positions(span_order, my_rank * local_rows, local_rows, span)
    start_state = (
        jnp.full((kv_heads, group, local_rows), -1e30, jnp.float32),
        jnp.zeros((kv_heads, group, local_rows), jnp.float32),
        jnp.zeros((kv_heads, group, local_rows, HD), jnp.float32),
    )

    def cycle_step(turn, state):
        carry, stacked = state
        source = (my_rank - turn) % ranks
        carry = attend_rows(
            carry, grouped, stacked[0], stacked[1], source * local_rows, query_pos, span_order, span
        )
        stacked = passed_along(stacked, "cp", 1)
        return (carry, stacked)

    stacked = jnp.stack([key_local, value_local])
    carry, stacked = lax.fori_loop(0, ranks - 1, cycle_step, (start_state, stacked))
    source = (my_rank - (ranks - 1)) % ranks
    carry = attend_rows(
        carry, grouped, stacked[0], stacked[1], source * local_rows, query_pos, span_order, span
    )
    running, total, summed = carry
    attended = (summed / total[..., None]).astype(jnp.bfloat16)
    attended = jnp.transpose(attended, (2, 0, 1, 3)).reshape(local_rows, kv_heads * group * HD)
    result = to_next(to_tokens(attended))
    return result[None]


def solution(mesh):
    in_specs = (P("pp", "cp", "tp"), P("pp", "cp", "tp"), P("pp", "cp", "tp"), P())
    out_specs = P("pp", ("cp", "tp"), None)
    return jax.shard_map(shards, mesh=mesh, in_specs=in_specs, out_specs=out_specs, check_vma=False)
```

profile of v0, /device:TPU:1, one launch (start us, length us, event | category | flops | bytes accessed | tf_op | source)
XLA Modules:
  0.0 147.3 jit_solution(13930984067491431697)
XLA Ops:
  0.0 0.7 select_reduce_fusion.2
  0.8 4.1 %copy.41 = bf16[1,256,4096]{1,2,0:T(8,128)(2,1)} copy(bf16[1,256,4096]{2,1,0:T(8,128)(2,1)} %param.10) | data formatting | bytes 4194304 | tf_op args[0]
  4.9 3.0 %copy.42 = bf16[256,4,8,128]{3,0,2,1:T(8,128)(2,1)S(1)} copy(bf16[256,4,8,128]{0,3,2,1:T(8,128)(2,1)} %bitcast.103) | data formatting | bytes 4194304 | tf_op jit(solution)/shard_map/while | solution.py:101
  8.0 0.1 copy.39
  8.1 0.1 copy.40
  8.3 0.8 pad_maximum_fusion
  9.1 2.4 %broadcast_in_dim.216 = f32[4,8,256,128]{3,2,1,0:T(8,128)} broadcast(f32[]{:T(128)} %constant.334.clone.1), dimensions={} | broadcast | bytes 4194308 | tf_op jit(solution)/shard_map/broadcast_in_dim | solution.py:88
  11.5 53.7 %while.79 = (s32[]{:T(128)}, f32[4,8,256]{2,1,0:T(8,128)S(1)}, f32[4,8,256]{2,1,0:T(8,128)S(1)}, f32[4,8,256,128]{3,2,1,0:T(8,128)}, bf16[2,256,512]{1,2,0:T(8,1...) while((s32[]{:T(128)}, f32[4,8,256]{2,1,0:T(8,128)S(1)}, ...), condition=%wide.region_7.8_spmd, body=%wide.region_1.7_spmd.sunk | while | flops 552655488 | bytes 28709564 | solution.py:101
  11.5 1.0 copy.82
  12.6 2.1 %collective-permute-start = (bf16[2,256,512]{1,2,0:T(8,128)(2,1)S(1)}, bf16[2,256,512]{1,2,0:T(8,128)(2,1)}, u32[]{:S(2)}, u32[]{:S(2)}) collective-permute-start(bf16[2,256,512]{1,2,0:T(8,128)(2,1)S(1)} %copy.82), channel_id=1, source_target_pairs={{0,2},{2,4},{4,6},{6,0},{1,3},{3,5},{5,7},{7,1},{8,10},{10,12},{12... | collective-permute-start | bytes 1572872 | tf_op jit(solution)/shard_map/while/body/eval_jaxpr/ppermute | solution.py:15
  14.8 15.2 %while.81 = (s32[]{:T(128)}, f32[4,8,256]{2,1,0:T(8,128)S(1)}, f32[4,8,256]{2,1,0:T(8,128)S(1)}, f32[4,8,256,128]{3,2,1,0:T(8,128)}, s32[]{:T(128)}, /*index=5*/...) while((s32[]{:T(128)}, f32[4,8,256]{2,1,0:T(8,128)S(1)}, ...), condition=%wide.region_6.6_spmd, body=%wide.region_2.5_spmd.sunk | while | flops 552655488 | bytes 24514796 | solution.py:62
  14.9 0.1 broadcast_compare_fusion.6
  15.0 0.9 fusion.61
  15.9 1.1 fusion.62
  17.1 5.3 %multiply_add_fusion.11 = f32[4,8,256,128]{3,2,1,0:T(8,128)} fusion(f32[4,8,256,128]{3,2,1,0:T(8,128)} %get-tuple-element.1191, bf16[128,4,128,1]{0,2,3,1:T(8,128)(2,1)S(1)} %bitcast.98, f32[4,128,256,8]{2,1,3,0:T(8,128)S(1)} %get-tuple-element.1170, f32[4,8,256]{2,1,0:T(8,128)S(1)} %get-tuple-element.1173, f32[4,8,256]{2,1,0:T(8,128)S(1)} %max.22, ...), kind=kOutput, calls=%fused_computation.1.clone.1 | convolution fusion | flops 275775488 | bytes 12812288 | tf_op jit(solution)/shard_map/while/body/eval_jaxpr/while/body/eval_jaxpr/ngqk,knd->ngqd/dot_general | solution.py:36
  22.4 0.1 select_reduce_fusion.6
  22.5 0.1 broadcast_compare_fusion.6
  22.6 0.9 fusion.61
  23.5 1.1 fusion.62
  24.6 5.3 %multiply_add_fusion.11 = f32[4,8,256,128]{3,2,1,0:T(8,128)} fusion(f32[4,8,256,128]{3,2,1,0:T(8,128)} %get-tuple-element.1191, bf16[128,4,128,1]{0,2,3,1:T(8,128)(2,1)S(1)} %bitcast.98, f32[4,128,256,8]{2,1,3,0:T(8,128)S(1)} %get-tuple-element.1170, f32[4,8,256]{2,1,0:T(8,128)S(1)} %get-tuple-element.1173, f32[4,8,256]{2,1,0:T(8,128)S(1)} %max.22, ...), kind=kOutput, calls=%fused_computation.1.clone.1 | convolution fusion | flops 275775488 | bytes 12812288 | tf_op jit(solution)/shard_map/while/body/eval_jaxpr/while/body/eval_jaxpr/ngqk,knd->ngqd/dot_general | solution.py:36
  30.0 1.0 copy.82
  31.0 1.3 collective-permute-start
  32.4 15.2 %while.81 = (s32[]{:T(128)}, f32[4,8,256]{2,1,0:T(8,128)S(1)}, f32[4,8,256]{2,1,0:T(8,128)S(1)}, f32[4,8,256,128]{3,2,1,0:T(8,128)}, s32[]{:T(128)}, /*index=5*/...) while((s32[]{:T(128)}, f32[4,8,256]{2,1,0:T(8,128)S(1)}, ...), condition=%wide.region_6.6_spmd, body=%wide.region_2.5_spmd.sunk | while | flops 552655488 | bytes 24514796 | solution.py:62
  32.4 0.1 select_reduce_fusion.6
  32.5 0.1 broadcast_compare_fusion.6
  32.6 0.9 fusion.61
  33.5 1.1 fusion.62
  34.7 5.3 %multiply_add_fusion.11 = f32[4,8,256,128]{3,2,1,0:T(8,128)} fusion(f32[4,8,256,128]{3,2,1,0:T(8,128)} %get-tuple-element.1191, bf16[128,4,128,1]{0,2,3,1:T(8,128)(2,1)S(1)} %bitcast.98, f32[4,128,256,8]{2,1,3,0:T(8,128)S(1)} %get-tuple-element.1170, f32[4,8,256]{2,1,0:T(8,128)S(1)} %get-tuple-element.1173, f32[4,8,256]{2,1,0:T(8,128)S(1)} %max.22, ...), kind=kOutput, calls=%fused_computation.1.clone.1 | convolution fusion | flops 275775488 | bytes 12812288 | tf_op jit(solution)/shard_map/while/body/eval_jaxpr/while/body/eval_jaxpr/ngqk,knd->ngqd/dot_general | solution.py:36
  40.0 0.1 select_reduce_fusion.6
  40.1 0.1 broadcast_compare_fusion.6
  40.2 0.9 fusion.61
  41.1 1.1 fusion.62
  42.3 5.3 %multiply_add_fusion.11 = f32[4,8,256,128]{3,2,1,0:T(8,128)} fusion(f32[4,8,256,128]{3,2,1,0:T(8,128)} %get-tuple-element.1191, bf16[128,4,128,1]{0,2,3,1:T(8,128)(2,1)S(1)} %bitcast.98, f32[4,128,256,8]{2,1,3,0:T(8,128)S(1)} %get-tuple-element.1170, f32[4,8,256]{2,1,0:T(8,128)S(1)} %get-tuple-element.1173, f32[4,8,256]{2,1,0:T(8,128)S(1)} %max.22, ...), kind=kOutput, calls=%fused_computation.1.clone.1 | convolution fusion | flops 275775488 | bytes 12812288 | tf_op jit(solution)/shard_map/while/body/eval_jaxpr/while/body/eval_jaxpr/ngqk,knd->ngqd/dot_general | solution.py:36
  47.6 1.0 copy.82
  48.6 1.3 collective-permute-start
  50.0 15.2 %while.81 = (s32[]{:T(128)}, f32[4,8,256]{2,1,0:T(8,128)S(1)}, f32[4,8,256]{2,1,0:T(8,128)S(1)}, f32[4,8,256,128]{3,2,1,0:T(8,128)}, s32[]{:T(128)}, /*index=5*/...) while((s32[]{:T(128)}, f32[4,8,256]{2,1,0:T(8,128)S(1)}, ...), condition=%wide.region_6.6_spmd, body=%wide.region_2.5_spmd.sunk | while | flops 552655488 | bytes 24514796 | solution.py:62
  50.1 0.1 broadcast_compare_fusion.6
  50.3 0.9 fusion.61
  51.2 1.1 fusion.62
  52.3 5.3 %multiply_add_fusion.11 = f32[4,8,256,128]{3,2,1,0:T(8,128)} fusion(f32[4,8,256,128]{3,2,1,0:T(8,128)} %get-tuple-element.1191, bf16[128,4,128,1]{0,2,3,1:T(8,128)(2,1)S(1)} %bitcast.98, f32[4,128,256,8]{2,1,3,0:T(8,128)S(1)} %get-tuple-element.1170, f32[4,8,256]{2,1,0:T(8,128)S(1)} %get-tuple-element.1173, f32[4,8,256]{2,1,0:T(8,128)S(1)} %max.22, ...), kind=kOutput, calls=%fused_computation.1.clone.1 | convolution fusion | flops 275775488 | bytes 12812288 | tf_op jit(solution)/shard_map/while/body/eval_jaxpr/while/body/eval_jaxpr/ngqk,knd->ngqd/dot_general | solution.py:36
  57.6 0.1 select_reduce_fusion.6
  57.7 0.1 broadcast_compare_fusion.6
  57.9 0.9 fusion.61
  58.7 1.1 fusion.62
  59.9 5.3 %multiply_add_fusion.11 = f32[4,8,256,128]{3,2,1,0:T(8,128)} fusion(f32[4,8,256,128]{3,2,1,0:T(8,128)} %get-tuple-element.1191, bf16[128,4,128,1]{0,2,3,1:T(8,128)(2,1)S(1)} %bitcast.98, f32[4,128,256,8]{2,1,3,0:T(8,128)S(1)} %get-tuple-element.1170, f32[4,8,256]{2,1,0:T(8,128)S(1)} %get-tuple-element.1173, f32[4,8,256]{2,1,0:T(8,128)S(1)} %max.22, ...), kind=kOutput, calls=%fused_computation.1.clone.1 | convolution fusion | flops 275775488 | bytes 12812288 | tf_op jit(solution)/shard_map/while/body/eval_jaxpr/while/body/eval_jaxpr/ngqk,knd->ngqd/dot_general | solution.py:36
  65.2 1.1 slice_bitcast_fusion.2
  66.3 15.2 %while.80 = (s32[]{:T(128)}, f32[4,8,256]{2,1,0:T(8,128)S(1)}, f32[4,8,256]{2,1,0:T(8,128)S(1)}, f32[4,8,256,128]{3,2,1,0:T(8,128)}, s32[]{:T(128)}, /*index=5*/...) while((s32[]{:T(128)}, f32[4,8,256]{2,1,0:T(8,128)S(1)}, ...), condition=%wide.region_12.13_spmd, body=%wide.region_8.12_spmd.sunk | while | flops 552655488 | bytes 24514796 | solution.py:62
  66.4 0.1 broadcast_compare_fusion.5
  66.5 0.9 fusion.54
  67.4 1.1 fusion.55
  68.6 5.3 %multiply_add_fusion.9 = f32[4,8,256,128]{3,2,1,0:T(8,128)} fusion(f32[4,8,256,128]{3,2,1,0:T(8,128)} %get-tuple-element.1287, bf16[128,4,128,1]{0,2,3,1:T(8,128)(2,1)S(1)} %bitcast.100, f32[4,128,256,8]{2,1,3,0:T(8,128)S(1)} %get-tuple-element.1154, f32[4,8,256]{2,1,0:T(8,128)S(1)} %get-tuple-element.1157, f32[4,8,256]{2,1,0:T(8,128)S(1)} %max.21, ...), kind=kOutput, calls=%fused_computation.31.clone.1 | convolution fusion | flops 275775488 | bytes 12812288 | tf_op jit(solution)/shard_map/while/body/eval_jaxpr/ngqk,knd->ngqd/dot_general | solution.py:36
  73.9 0.1 select_reduce_fusion.5
  74.0 0.1 broadcast_compare_fusion.5
  74.1 0.9 fusion.54
  75.0 1.1 fusion.55
  76.2 5.3 %multiply_add_fusion.9 = f32[4,8,256,128]{3,2,1,0:T(8,128)} fusion(f32[4,8,256,128]{3,2,1,0:T(8,128)} %get-tuple-element.1287, bf16[128,4,128,1]{0,2,3,1:T(8,128)(2,1)S(1)} %bitcast.100, f32[4,128,256,8]{2,1,3,0:T(8,128)S(1)} %get-tuple-element.1154, f32[4,8,256]{2,1,0:T(8,128)S(1)} %get-tuple-element.1157, f32[4,8,256]{2,1,0:T(8,128)S(1)} %max.21, ...), kind=kOutput, calls=%fused_computation.31.clone.1 | convolution fusion | flops 275775488 | bytes 12812288 | tf_op jit(solution)/shard_map/while/body/eval_jaxpr/ngqk,knd->ngqd/dot_general | solution.py:36
  81.5 2.9 %fusion.26 = bf16[256,4,8,128]{3,0,2,1:T(8,128)(2,1)S(1)} fusion(f32[4,8,256,128]{3,2,1,0:T(8,128)} %get-tuple-element.809, f32[4,8,256]{2,1,0:T(8,128)S(1)} %get-tuple-element.810), kind=kLoop, calls=%fused_computation.59 | loop fusion | flops 2097152 | bytes 6324224 | tf_op jit(solution)/shard_map/transpose | solution.py:108
  84.3 1.4 copy.44
  85.7 2.3 %all_to_all.14 = bf16[2,128,4096]{2,1,0:T(8,128)(2,1)} reshape(bf16[256,4,8,128]{3,2,1,0:T(8,128)(2,1)S(1)} %copy.44) | data formatting | bytes 4194304 | tf_op jit(solution)/shard_map/all_to_all | solution.py:66
  88.0 27.1 %all_to_all.19 = bf16[2,128,4096]{2,1,0:T(8,128)(2,1)S(1)} all-to-all(bf16[2,128,4096]{2,1,0:T(8,128)(2,1)} %all_to_all.14), channel_id=1, replica_groups=mesh['pp'=4,'cp'=4,'tp'=2] {'tp'}, dimensions={0} | all-to-all | bytes 4194304 | tf_op jit(solution)/shard_map/all_to_all | solution.py:66
  115.1 2.4 %copy.45 = bf16[128,2,4096]{0,2,1:T(8,128)(2,1)} copy(bf16[128,2,4096]{2,0,1:T(8,128)(2,1)S(1)} %bitcast.102) | data formatting | bytes 4194304 | tf_op jit(solution)/shard_map/all_to_all | solution.py:66
  117.5 3.6 %collective-permute-start.1 = (bf16[128,8192]{0,1:T(8,128)(2,1)}, bf16[128,8192]{0,1:T(8,128)(2,1)S(1)}, u32[]{:S(2)}, u32[]{:S(2)}) collective-permute-start(bf16[128,8192]{0,1:T(8,128)(2,1)} %bitcast.104), channel_id=1, source_target_pairs={{0,8},{8,16},{16,24},{24,0},{1,9},{9,17},{17,25},{25,1},{2,10},{10... | collective-permute-start | bytes 6291464 | tf_op jit(solution)/shard_map/ppermute | solution.py:15
  121.1 23.3 %collective-permute-done.1 = bf16[128,8192]{0,1:T(8,128)(2,1)S(1)} collective-permute-done((bf16[128,8192]{0,1:T(8,128)(2,1)}, bf16[128,8192]{0,1:T(8,128)(2,1)S(1)}, u32[]{:S(2)}, u32[]{:S(2)}) %collective-permute-start.1) | collective-permute-done | bytes 2097184 | tf_op jit(solution)/shard_map/ppermute | solution.py:15
  144.4 2.9 %copy.46 = bf16[1,128,8192]{2,1,0:T(8,128)(2,1)} copy(bf16[1,128,8192]{1,2,0:T(8,128)(2,1)S(1)} %bitcast.105) | data formatting | bytes 4194304 | tf_op jit(solution)/shard_map/broadcast_in_dim | solution.py:110
  (67 shorter events, 1.1 us)
Async XLA Ops:
  0.8 7.2 %copy-start = (bf16[1,256,512]{2,1,0:T(8,128)(2,1)S(1)}, bf16[1,256,512]{2,1,0:T(8,128)(2,1)}, u32[]{:S(2)}) copy-start(bf16[1,256,512]{2,1,0:T(8,128)(2,1)} %param.11) | copy-start | bytes 786436
  0.8 7.3 %copy-start.1 = (bf16[1,256,512]{2,1,0:T(8,128)(2,1)S(1)}, bf16[1,256,512]{2,1,0:T(8,128)(2,1)}, u32[]{:S(2)}) copy-start(bf16[1,256,512]{2,1,0:T(8,128)(2,1)} %param.12) | copy-start | bytes 786436
  8.0 3.6 %copy-start.2 = (s32[8]{0:T(128)S(1)}, s32[8]{0:T(128)}, u32[]{:S(2)}) copy-start(s32[8]{0:T(128)} %param.13) | copy-start | bytes 100
  12.6 17.4 %collective-permute-start = (bf16[2,256,512]{1,2,0:T(8,128)(2,1)S(1)}, bf16[2,256,512]{1,2,0:T(8,128)(2,1)}, u32[]{:S(2)}, u32[]{:S(2)}) collective-permute-start(bf16[2,256,512]{1,2,0:T(8,128)(2,1)S(1)} %copy.82), channel_id=1, source_target_pairs={{0,2},{2,4},{4,6},{6,0},{1,3},{3,5},{5,7},{7,1},{8,10},{10,12},{12... | collective-permute-start | bytes 1572872 | tf_op jit(solution)/shard_map/while/body/eval_jaxpr/ppermute | solution.py:15
  31.0 16.6 %collective-permute-start = (bf16[2,256,512]{1,2,0:T(8,128)(2,1)S(1)}, bf16[2,256,512]{1,2,0:T(8,128)(2,1)}, u32[]{:S(2)}, u32[]{:S(2)}) collective-permute-start(bf16[2,256,512]{1,2,0:T(8,128)(2,1)S(1)} %copy.82), channel_id=1, source_target_pairs={{0,2},{2,4},{4,6},{6,0},{1,3},{3,5},{5,7},{7,1},{8,10},{10,12},{12... | collective-permute-start | bytes 1572872 | tf_op jit(solution)/shard_map/while/body/eval_jaxpr/ppermute | solution.py:15
  48.6 16.6 %collective-permute-start = (bf16[2,256,512]{1,2,0:T(8,128)(2,1)S(1)}, bf16[2,256,512]{1,2,0:T(8,128)(2,1)}, u32[]{:S(2)}, u32[]{:S(2)}) collective-permute-start(bf16[2,256,512]{1,2,0:T(8,128)(2,1)S(1)} %copy.82), channel_id=1, source_target_pairs={{0,2},{2,4},{4,6},{6,0},{1,3},{3,5},{5,7},{7,1},{8,10},{10,12},{12... | collective-permute-start | bytes 1572872 | tf_op jit(solution)/shard_map/while/body/eval_jaxpr/ppermute | solution.py:15
  117.5 26.8 %collective-permute-start.1 = (bf16[128,8192]{0,1:T(8,128)(2,1)}, bf16[128,8192]{0,1:T(8,128)(2,1)S(1)}, u32[]{:S(2)}, u32[]{:S(2)}) collective-permute-start(bf16[128,8192]{0,1:T(8,128)(2,1)} %bitcast.104), channel_id=1, source_target_pairs={{0,8},{8,16},{16,24},{24,0},{1,9},{9,17},{17,25},{25,1},{2,10},{10... | collective-permute-start | bytes 6291464 | tf_op jit(solution)/shard_map/ppermute | solution.py:15
where the time goes:
time: 149 us; the launch traced here: 147 us
  matrix products  49.5 us (33%)
  blocking collectives  27.1 us (18%)
  local copies, waits for them, and re-layouts  23.4 us (16%)
  waiting for transfers between devices  23.3 us (16%)
  other arithmetic  15 us (10%)
  starting transfers between devices  8.28 us (6%)
    dot_general x8, matrix products, attend_block(): jnp.einsum('ngqk,knd->ngqd', weight.astype(jnp.bfloat16), value_rows, pre...  42.5 us
    all_to_all x1, blocking collectives, to_tokens(): lax.all_to_all(attended, 'tp', split_axis=0, concat_axis=1, tiled=True)  27.1 us
    ppermute x4, waiting for transfers between devices, passed_along(): return lax.ppermute(value, axis, pairs)  23.3 us
    reduce_sum x8, other arithmetic, attend_block(): total = total * fade + jnp.sum(weight, axis=-1)  8.74 us
    ppermute x4, starting transfers between devices, passed_along(): return lax.ppermute(value, axis, pairs)  8.28 us
    dot_general x8, matrix products, attend_block(): jnp.einsum('qngd,knd->ngqk', grouped, key_rows, preferred_element_type=jn...  6.99 us
    all_to_all x2, local copies, waits for them, and re-layouts, to_tokens(): lax.all_to_all(attended, 'tp', split_axis=0, concat_axis=1, tiled=True)  4.73 us
    unnamed x9, local copies, waits for them, and re-layouts  4.41 us
  transfers between devices with their start and end apart: 4, of which 1 were waited for; matrix products, arithmetic and copies ran while one was open for 31% of the time, Pallas kernels for 0%

commit v1 on v0

v1 whole, which is shorter than its diff:
```python
import functools
import math

import jax
import jax.numpy as jnp
from jax import lax
from jax.experimental import pallas as pl
from jax.experimental.pallas import tpu as pltpu
from jax.sharding import PartitionSpec as P

HD = 128
SPAN = 128
MESH = pl.DeviceIdType.MESH


def kernel(
    n, tps, pps, kv_heads, group, pieces,
    order_ref, q_ref, k_ref, v_ref, out_ref,
    qbuf, kvbuf, obuf, bias,
    qsem, lsem, right_send, right_recv, left_send, left_recv, out_send, out_recv,
):
    rows = q_ref.shape[0]
    me = lax.axis_index("cp")
    my_tp = lax.axis_index("tp")
    my_pp = lax.axis_index("pp")
    next_pp = lax.rem(my_pp + 1, pps)
    last_pp = lax.rem(my_pp + pps - 1, pps)
    part = rows // tps
    width = group * HD
    per_piece = group // pieces
    piece_width = per_piece * HD

    own = []
    for h in range(kv_heads):
        for which, ref in enumerate((k_ref, v_ref)):
            copy = pltpu.make_async_copy(
                ref.at[:, pl.ds(h * HD, HD)], kvbuf.at[h, me, which], lsem.at[h, which]
            )
            copy.start()
            own.append(copy)
    q_copies = []
    for h in range(kv_heads):
        copy = pltpu.make_async_copy(
            q_ref.at[:, pl.ds(h * width, width)], qbuf.at[:, pl.ds(h * width, width)], qsem.at[h]
        )
        copy.start()
        q_copies.append(copy)

    barrier = pltpu.get_barrier_semaphore()

    @pl.when(me > 0)
    def _():
        pl.semaphore_signal(barrier, inc=1, device_id={"cp": me - 1}, device_id_type=MESH)

    @pl.when(me < n - 1)
    def _():
        pl.semaphore_signal(barrier, inc=1, device_id={"cp": me + 1}, device_id_type=MESH)

    for t in range(tps):
        for other in (next_pp, last_pp):
            pl.semaphore_signal(
                barrier, inc=1, device_id={"pp": other, "tp": t}, device_id_type=MESH
            )
    near = jnp.where(me > 0, 1, 0) + jnp.where(me < n - 1, 1, 0)
    pl.semaphore_wait(barrier, 2 * tps + near)

    def to_right(h, k):
        slot = me - k
        return pltpu.make_async_remote_copy(
            src_ref=kvbuf.at[h, slot], dst_ref=kvbuf.at[h, slot],
            send_sem=right_send.at[h, k], recv_sem=right_recv.at[h, k],
            device_id={"cp": me + 1}, device_id_type=MESH,
        )

    def to_left(h, k):
        slot = me + k
        return pltpu.make_async_remote_copy(
            src_ref=kvbuf.at[h, slot], dst_ref=kvbuf.at[h, slot],
            send_sem=left_send.at[h, k], recv_sem=left_recv.at[h, k],
            device_id={"cp": me - 1}, device_id_type=MESH,
        )

    def from_left(h, k):
        return pltpu.make_async_remote_copy(
            src_ref=kvbuf.at[h, me - k], dst_ref=kvbuf.at[h, me - k],
            send_sem=right_send.at[h, k - 1], recv_sem=right_recv.at[h, k - 1],
            device_id={"cp": me - 1}, device_id_type=MESH,
        )

    def from_right(h, k):
        return pltpu.make_async_remote_copy(
            src_ref=kvbuf.at[h, me + k], dst_ref=kvbuf.at[h, me + k],
            send_sem=left_send.at[h, k - 1], recv_sem=left_recv.at[h, k - 1],
            device_id={"cp": me + 1}, device_id_type=MESH,
        )

    def send_own(h):
        own[2 * h].wait()
        own[2 * h + 1].wait()

        @pl.when(me < n - 1)
        def _():
            to_right(h, 0).start()

        @pl.when(me > 0)
        def _():
            to_left(h, 0).start()

    def take(h, k):
        @pl.when(me - k >= 0)
        def _():
            from_left(h, k).wait_recv()

            @pl.when(me < n - 1)
            def _():
                to_right(h, k).start()

        @pl.when(me + k <= n - 1)
        def _():
            from_right(h, k).wait_recv()

            @pl.when(me > 0)
            def _():
                to_left(h, k).start()

    def out_copy(h, piece, t):
        first = h * width + piece * piece_width
        index = (h * pieces + piece) * tps
        return pltpu.make_async_remote_copy(
            src_ref=obuf.at[pl.ds(t * part, part), pl.ds(first, piece_width)],
            dst_ref=out_ref.at[:, pl.ds(my_tp * kv_heads * width + first, piece_width)],
            send_sem=out_send.at[index + t], recv_sem=out_recv.at[index + my_tp],
            device_id={"pp": next_pp, "tp": t}, device_id_type=MESH,
        )

    def out_arrival(h, piece, t):
        first = h * width + piece * piece_width
        index = (h * pieces + piece) * tps
        return pltpu.make_async_remote_copy(
            src_ref=obuf.at[pl.ds(0, part), pl.ds(first, piece_width)],
            dst_ref=out_ref.at[:, pl.ds(t * kv_heads * width + first, piece_width)],
            send_sem=out_send.at[index + t], recv_sem=out_recv.at[index + t],
            device_id={"pp": last_pp, "tp": t}, device_id_type=MESH,
        )

    send_own(0)
    if kv_heads > 1:
        send_own(1)

    spans = rows // SPAN
    row_in = lax.broadcasted_iota(jnp.int32, (SPAN, SPAN), 0)
    col_in = lax.broadcasted_iota(jnp.int32, (SPAN, SPAN), 1)
    for i in range(spans):
        query_span = order_ref[me * spans + i]

        def mask_span(j, _):
            gap = (query_span - order_ref[j]) * SPAN
            seen = col_in - row_in <= gap
            bias[j, pl.ds(i * SPAN, SPAN), :] = jnp.where(seen, 0.0, -1e30).astype(jnp.float32)
            return 0

        lax.fori_loop(0, n * spans, mask_span, 0)

    keys_all = n * rows

    def attend(h, piece):
        def one_head(g, _):
            first = pl.multiple_of(h * width + (piece * per_piece + g) * HD, HD)
            query = qbuf[:, pl.ds(first, HD)]
            key = kvbuf[h, :, 0].reshape(keys_all, HD)
            value = kvbuf[h, :, 1].reshape(keys_all, HD)
            score = lax.dot_general(
                query, key, (((1,), (1,)), ((), ())), preferred_element_type=jnp.float32
            )
            mask = jnp.concatenate([bias[j] for j in range(n * spans)], axis=1)
            score = score * (1.0 / HD**0.5) + mask
            top = jnp.max(score, axis=1, keepdims=True)
            weight = jnp.exp(score - top)
            total = jnp.sum(weight, axis=1, keepdims=True)
            mixed = jnp.dot(weight.astype(jnp.bfloat16), value, preferred_element_type=jnp.float32)
            obuf[:, pl.ds(first, HD)] = (mixed / total).astype(jnp.bfloat16)
            return 0

        lax.fori_loop(0, per_piece, one_head, 0)

    for h in range(kv_heads):
        for k in range(1, n):
            if h == 0 or k > 1:
                take(h, k)
            if k == 1 and h + 2 < kv_heads:
                send_own(h + 2)
        q_copies[h].wait()
        for piece in range(pieces):
            attend(h, piece)
            if piece == 0 and h + 1 < kv_heads:
                take(h + 1, 1)
            for t in range(tps):
                out_copy(h, piece, t).start()

    for h in range(kv_heads):
        for k in range(n - 1):
            @pl.when((me - k >= 0) & (me < n - 1))
            def _():
                to_right(h, k).wait_send()

            @pl.when((me + k <= n - 1) & (me > 0))
            def _():
                to_left(h, k).wait_send()

    for h in range(kv_heads):
        for piece in range(pieces):
            for t in range(tps):
                out_copy(h, piece, t).wait_send()
                out_arrival(h, piece, t).wait_recv()


def shards(queries, keys, values, span_order):
    query_rows, key_local, value_local = queries[0], keys[0], values[0]
    rows = query_rows.shape[0]
    kv_heads = key_local.shape[1] // HD
    group = query_rows.shape[1] // HD // kv_heads
    n, tps, pps = lax.axis_size("cp"), lax.axis_size("tp"), lax.axis_size("pp")
    pieces = 2
    copies = kv_heads * pieces * tps
    dma = pltpu.SemaphoreType.DMA
    result = pl.pallas_call(
        functools.partial(kernel, n, tps, pps, kv_heads, group, pieces),
        out_shape=jax.ShapeDtypeStruct((rows // tps, tps * query_rows.shape[1]), jnp.bfloat16),
        in_specs=[
            pl.BlockSpec(memory_space=pltpu.SMEM),
            pl.BlockSpec(memory_space=pl.ANY),
            pl.BlockSpec(memory_space=pl.ANY),
            pl.BlockSpec(memory_space=pl.ANY),
        ],
        out_specs=pl.BlockSpec(memory_space=pl.ANY),
        scratch_shapes=[
            pltpu.VMEM(query_rows.shape, jnp.bfloat16),
            pltpu.VMEM((kv_heads, n, 2, rows, HD), jnp.bfloat16),
            pltpu.VMEM(query_rows.shape, jnp.bfloat16),
            pltpu.VMEM((n * rows // SPAN, rows, SPAN), jnp.float32),
            dma((kv_heads,)),
            dma((kv_heads, 2)),
            dma((kv_heads, n)),
            dma((kv_heads, n)),
            dma((kv_heads, n)),
            dma((kv_heads, n)),
            dma((copies,)),
            dma((copies,)),
        ],
        compiler_params=pltpu.CompilerParams(
            collective_id=0, has_side_effects=True, vmem_limit_bytes=56 * 1024 * 1024
        ),
    )(span_order, query_rows, key_local, value_local)
    return result[None]


def solution(mesh):
    in_specs = (P("pp", "cp", "tp"), P("pp", "cp", "tp"), P("pp", "cp", "tp"), P())
    out_specs = P("pp", ("cp", "tp"), None)
    return jax.shard_map(shards, mesh=mesh, in_specs=in_specs, out_specs=out_specs, check_vma=False)
```

time: 149 us -> 54.3 us (0.36); the launches traced: 147 us -> 54.1 us
  Pallas kernels: 0 us -> 51 us
  matrix products: 49.5 us -> 0 us
  blocking collectives: 27.1 us -> 0 us
  waiting for transfers between devices: 23.3 us -> 0 us
  local copies, waits for them, and re-layouts: 23.4 us -> 3.1 us
  other arithmetic: 15 us -> 0 us
  starting transfers between devices: 8.28 us -> 0 us
    pallas_call x0 -> x1, Pallas kernels: none -> 51 us  [shards(): pl.pallas_call(functools.partial(kernel, n, tps, pps, kv_heads, group, pi...]
    dot_general x16 -> x0, matrix products: 49.5 us -> none  [the longest x8 42.5 us: attend_block(): jnp.einsum('ngqk,knd->ngqd', weight.astype(jnp.bfloat16), value_rows, pre...]
    all_to_all x1 -> x0, blocking collectives: 27.1 us -> none  [to_tokens(): lax.all_to_all(attended, 'tp', split_axis=0, concat_axis=1, tiled=True)]
    ppermute x4 -> x0, waiting for transfers between devices: 23.3 us -> none  [passed_along(): return lax.ppermute(value, axis, pairs)]
    reduce_sum x17 -> x0, other arithmetic: 10.2 us -> none  [the longest x8 8.74 us: attend_block(): total = total * fade + jnp.sum(weight, axis=-1)]
    ppermute x4 -> x0, starting transfers between devices: 8.28 us -> none  [passed_along(): return lax.ppermute(value, axis, pairs)]
    broadcast_in_dim x4 -> x0, local copies, waits for them, and re-layouts: 5.3 us -> none  [the longest x1 2.88 us: shards(): return result[None]]
    all_to_all x2 -> x0, local copies, waits for them, and re-layouts: 4.73 us -> none  [to_tokens(): lax.all_to_all(attended, 'tp', split_axis=0, concat_axis=1, tiled=True)]
  transfers between devices with their start and end apart: 4 -> 0, of which waited for: 1 -> 0; matrix products, arithmetic and copies ran while one was open for 31% -> 0% of each run, Pallas kernels for 0% -> 0%
where the time goes in v1:
time: 54.3 us; the launch traced here: 54.1 us
  Pallas kernels  51 us (94%)
  local copies, waits for them, and re-layouts  3.1 us (6%)
    pallas_call x1, Pallas kernels, shards(): pl.pallas_call(functools.partial(kernel, n, tps, pps, kv_heads, group, pi...  51 us
    unnamed x1, local copies, waits for them, and re-layouts  3.1 us

profile of v1, /device:TPU:1, one launch (start us, length us, event | category | flops | bytes accessed | tf_op | source)
XLA Modules:
  0.0 54.1 jit_solution(573399322102317741)
XLA Ops:
  0.0 51.0 %shard_map.46 = bf16[128,8192]{1,0:T(8,128)(2,1)} custom-call(s32[8]{0:T(128)} %order_ref.1, bf16[256,4096]{1,0:T(8,128)(2,1)} %bitcast.5, bf16[256,512]{1,0:T(8,128)(2,1)} %bitcast.6, bf16[256,512]{1,0:T(8,128)(2,1)} %bitcast.7), custom_call_target="tpu_custom_call" | custom-call | tf_op jit(solution)/shard_map/pallas_call | solution.py:226
  51.0 3.1 %copy.6 = bf16[1,128,8192]{2,1,0:T(8,128)(2,1)} copy(bf16[1,128,8192]{2,1,0:T(8,128)(2,1)} %bitcast.4) | data formatting | bytes 4194304

commit v2 on v1

--- a/solution.py
+++ b/solution.py
@@ -10,13 +10,14 @@
 
 HD = 128
 SPAN = 128
+LOG_SCALE = math.log2(math.e) / math.sqrt(HD)
 MESH = pl.DeviceIdType.MESH
 
 
 def kernel(
-    n, tps, pps, kv_heads, group, pieces,
+    n, tps, pps, kv_heads, group,
     order_ref, q_ref, k_ref, v_ref, out_ref,
-    qbuf, kvbuf, obuf, bias,
+    qbuf, kvbuf, obuf, bias, score_a, score_b, part_mixed, part_top, part_total,
     qsem, lsem, right_send, right_recv, left_send, left_recv, out_send, out_recv,
 ):
     rows = q_ref.shape[0]
@@ -27,8 +28,8 @@
     last_pp = lax.rem(my_pp + pps - 1, pps)
     part = rows // tps
     width = group * HD
-    per_piece = group // pieces
-    piece_width = per_piece * HD
+    pieces = group // 2
+    piece_width = 2 * HD
 
     own = []
     for h in range(kv_heads):
@@ -123,18 +124,21 @@
             def _():
                 to_left(h, k).start()
 
+    def take_far(h):
+        take(h, n - 1)
+
     def out_copy(h, piece, t):
-        first = h * width + piece * piece_width
+        first = pl.multiple_of(h * width + piece * piece_width, HD)
         index = (h * pieces + piece) * tps
         return pltpu.make_async_remote_copy(
             src_ref=obuf.at[pl.ds(t * part, part), pl.ds(first, piece_width)],
-            dst_ref=out_ref.at[:, pl.ds(my_tp * kv_heads * width + first, piece_width)],
+            dst_ref=out_ref.at[:, pl.ds(pl.multiple_of(my_tp * kv_heads * width + first, HD), piece_width)],
             send_sem=out_send.at[index + t], recv_sem=out_recv.at[index + my_tp],
             device_id={"pp": next_pp, "tp": t}, device_id_type=MESH,
         )
 
     def out_arrival(h, piece, t):
-        first = h * width + piece * piece_width
+        first = pl.multiple_of(h * width + piece * piece_width, HD)
         index = (h * pieces + piece) * tps
         return pltpu.make_async_remote_copy(
             src_ref=obuf.at[pl.ds(0, part), pl.ds(first, piece_width)],
@@ -161,41 +165,111 @@
 
         lax.fori_loop(0, n * spans, mask_span, 0)
 
-    keys_all = n * rows
-
-    def attend(h, piece):
-        def one_head(g, _):
-            first = pl.multiple_of(h * width + (piece * per_piece + g) * HD, HD)
-            query = qbuf[:, pl.ds(first, HD)]
-            key = kvbuf[h, :, 0].reshape(keys_all, HD)
-            value = kvbuf[h, :, 1].reshape(keys_all, HD)
-            score = lax.dot_general(
-                query, key, (((1,), (1,)), ((), ())), preferred_element_type=jnp.float32
-            )
-            mask = jnp.concatenate([bias[j] for j in range(n * spans)], axis=1)
-            score = score * (1.0 / HD**0.5) + mask
+    low = jnp.where(me < n // 2, 0, 1)
+    far = jnp.where(me < n // 2, n - 1, 0)
+    inner = (me > 0) & (me < n - 1)
+
+    def block(h, slot, count, which):
+        return kvbuf[h, pl.ds(slot, count), which].reshape(count * rows, HD)
+
+    def head_columns(h, g):
+        return pl.ds(pl.multiple_of(h * width + g * HD, HD), HD)
+
+    def score_of(h, g, slot, count):
+        return lax.dot_general(
+            qbuf[:, head_columns(h, g)], block(h, slot, count, 0),
+            (((1,), (1,)), ((), ())), preferred_element_type=jnp.float32,
+        )
+
+    def masked(score, slot, count):
+        masks = [bias[slot * spans + j] for j in range(count * spans)]
+        return score + jnp.concatenate(masks, axis=1)
+
+    def weigh(h, score, top, slot, count):
+        weight = jnp.exp2((score - top) * LOG_SCALE)
+        total = jnp.sum(weight, axis=1, keepdims=True)
+        mixed = jnp.dot(
+            weight.astype(jnp.bfloat16), block(h, slot, count, 1),
+            preferred_element_type=jnp.float32,
+        )
+        return mixed, total
+
+    def finish(h, g, mixed, total):
+        obuf[:, head_columns(h, g)] = (mixed / total).astype(jnp.bfloat16)
+
+    def send_piece(h, piece):
+        for t in range(tps):
+            out_copy(h, piece, t).start()
+
+    def pairs(h, slot, count, done, between):
+        score_a[:, : count * rows] = score_of(h, 0, slot, count)
+
+        def pair(i, _):
+            score_b[:, : count * rows] = score_of(h, 2 * i + 1, slot, count)
+            done(2 * i, masked(score_a[:, : count * rows], slot, count))
+            following = jnp.minimum(2 * i + 2, group - 1)
+            score_a[:, : count * rows] = score_of(h, following, slot, count)
+            done(2 * i + 1, masked(score_b[:, : count * rows], slot, count))
+            between(i)
+            return 0
+
+        lax.fori_loop(0, group // 2, pair, 0)
+
+    def whole_head(h):
+        def done(g, score):
             top = jnp.max(score, axis=1, keepdims=True)
-            weight = jnp.exp(score - top)
-            total = jnp.sum(weight, axis=1, keepdims=True)
-            mixed = jnp.dot(weight.astype(jnp.bfloat16), value, preferred_element_type=jnp.float32)
-            obuf[:, pl.ds(first, HD)] = (mixed / total).astype(jnp.bfloat16)
+            finish(h, g, *weigh(h, score, top, 0, n))
+
+        def between(i):
+            send_piece(h, i)
+            for k in range(1, n - 1):
+                @pl.when((i == min(k - 1, group // 2 - 1)) & inner)
+                def _():
+                    take(h + 1, k)
+
+        pairs(h, 0, n, done, between)
+
+    def last_head(h):
+        def done(g, score):
+            top = jnp.max(score, axis=1, keepdims=True)
+            mixed, total = weigh(h, score, top, low, n - 1)
+            part_mixed[g] = mixed
+            part_top[g] = jnp.broadcast_to(top, (rows, HD))
+            part_total[g] = jnp.broadcast_to(total, (rows, HD))
+
+        pairs(h, low, n - 1, done, lambda i: None)
+        take_far(h)
+
+        def pair(i, _):
+            for g in (2 * i, 2 * i + 1):
+                score = masked(score_of(h, g, far, 1), far, 1)
+                before = part_top[g]
+                top = jnp.maximum(before, jnp.max(score, axis=1, keepdims=True))
+                fade = jnp.exp2((before - top) * LOG_SCALE)
+                mixed, total = weigh(h, score, top[:, :1], far, 1)
+                finish(h, g, part_mixed[g] * fade + mixed, part_total[g] * fade + total)
+            send_piece(h, i)
             return 0
 
-        lax.fori_loop(0, per_piece, one_head, 0)
-
-    for h in range(kv_heads):
-        for k in range(1, n):
-            if h == 0 or k > 1:
+        lax.fori_loop(0, group // 2, pair, 0)
+
+    for h in range(kv_heads):
+        ends = jnp.logical_not(inner)
+        if h == 0:
+            ends = me >= 0
+        for k in range(1, n - 1):
+            @pl.when(ends)
+            def _():
                 take(h, k)
+
             if k == 1 and h + 2 < kv_heads:
                 send_own(h + 2)
         q_copies[h].wait()
-        for piece in range(pieces):
-            attend(h, piece)
-            if piece == 0 and h + 1 < kv_heads:
-                take(h + 1, 1)
-            for t in range(tps):
-                out_copy(h, piece, t).start()
+        if h < kv_heads - 1:
+            take_far(h)
+            whole_head(h)
+        else:
+            last_head(h)
 
     for h in range(kv_heads):
         for k in range(n - 1):
@@ -208,10 +282,17 @@
                 to_left(h, k).wait_send()
 
     for h in range(kv_heads):
-        for piece in range(pieces):
+        def drain(piece, _):
             for t in range(tps):
                 out_copy(h, piece, t).wait_send()
                 out_arrival(h, piece, t).wait_recv()
+            return 0
+
+        lax.fori_loop(0, pieces, drain, 0)
+
+
+def place(x_ref, o_ref):
+    o_ref[...] = x_ref[...]
 
 
 def shards(queries, keys, values, span_order):
@@ -220,11 +301,10 @@
     kv_heads = key_local.shape[1] // HD
     group = query_rows.shape[1] // HD // kv_heads
     n, tps, pps = lax.axis_size("cp"), lax.axis_size("tp"), lax.axis_size("pp")
-    pieces = 2
-    copies = kv_heads * pieces * tps
+    copies = kv_heads * (group // 2) * tps
     dma = pltpu.SemaphoreType.DMA
     result = pl.pallas_call(
-        functools.partial(kernel, n, tps, pps, kv_heads, group, pieces),
+        functools.partial(kernel, n, tps, pps, kv_heads, group),
         out_shape=jax.ShapeDtypeStruct((rows // tps, tps * query_rows.shape[1]), jnp.bfloat16),
         in_specs=[
             pl.BlockSpec(memory_space=pltpu.SMEM),
@@ -238,6 +318,11 @@
             pltpu.VMEM((kv_heads, n, 2, rows, HD), jnp.bfloat16),
             pltpu.VMEM(query_rows.shape, jnp.bfloat16),
             pltpu.VMEM((n * rows // SPAN, rows, SPAN), jnp.float32),
+            pltpu.VMEM((rows, n * rows), jnp.float32),
+            pltpu.VMEM((rows, n * rows), jnp.float32),
+            pltpu.VMEM((group, rows, HD), jnp.float32),
+            pltpu.VMEM((group, rows, HD), jnp.float32),
+            pltpu.VMEM((group, rows, HD), jnp.float32),
             dma((kv_heads,)),
             dma((kv_heads, 2)),
             dma((kv_heads, n)),
@@ -251,7 +336,16 @@
             collective_id=0, has_side_effects=True, vmem_limit_bytes=56 * 1024 * 1024
         ),
     )(span_order, query_rows, key_local, value_local)
-    return result[None]
+    columns = result.shape[1] // 8
+    spec = pl.BlockSpec((result.shape[0], columns), lambda i: (0, i))
+    placed = pl.pallas_call(
+        place,
+        grid=(8,),
+        out_shape=jax.ShapeDtypeStruct(result.shape, result.dtype),
+        in_specs=[spec],
+        out_specs=spec,
+    )(result)
+    return placed[None]
 
 
 def solution(mesh):

time: 54.3 us -> 57.4 us (1.057)
  Pallas kernels: 51 us -> 57.1 us
  local copies, waits for them, and re-layouts: 3.1 us -> 0 us
    pallas_call x1 -> x2, Pallas kernels: 51 us -> 57.1 us  [the longest x1 51.5 us: shards(): pl.pallas_call(functools.partial(kernel, n, tps, pps, kv_heads, group), o...]
    unnamed x1 -> x0, local copies, waits for them, and re-layouts: 3.1 us -> none
where the time goes in v2:
time: 57.4 us; the launch traced here: 57.1 us
  Pallas kernels  57.1 us (99%)
    pallas_call x1, Pallas kernels, shards(): pl.pallas_call(functools.partial(kernel, n, tps, pps, kv_heads, group), o...  51.5 us
    pallas_call x1, Pallas kernels, shards(): pl.pallas_call(place, grid=(8,), out_shape=jax.ShapeDtypeStruct(result.sh...  5.64 us

profile of v2, /device:TPU:1, one launch (start us, length us, event | category | flops | bytes accessed | tf_op | source)
XLA Modules:
  0.0 57.1 jit_solution(12372217246067627915)
XLA Ops:
  0.0 51.5 %shard_map.46.x_ref = bf16[128,8192]{1,0:T(8,128)(2,1)} custom-call(s32[8]{0:T(128)} %order_ref.1, bf16[256,4096]{1,0:T(8,128)(2,1)} %bitcast.4, bf16[256,512]{1,0:T(8,128)(2,1)} %bitcast.5, bf16[256,512]{1,0:T(8,128)(2,1)} %bitcast.6), custom_call_target="tpu_custom_call" | custom-call | tf_op jit(solution)/shard_map/pallas_call | solution.py:306
  51.5 5.6 %shard_map.47 = bf16[128,8192]{1,0:T(8,128)(2,1)} custom-call(bf16[128,8192]{1,0:T(8,128)(2,1)} %shard_map.46.x_ref), custom_call_target="tpu_custom_call" | custom-call | tf_op jit(solution)/shard_map/pallas_call | solution.py:341

commit v3 on v2

--- a/solution.py
+++ b/solution.py
@@ -95,15 +95,17 @@
             device_id={"cp": me + 1}, device_id_type=MESH,
         )
 
-    def send_own(h):
-        own[2 * h].wait()
-        own[2 * h + 1].wait()
-
-        @pl.when(me < n - 1)
+    def send_own(h, inward):
+        if not inward:
+            own[2 * h].wait()
+            own[2 * h + 1].wait()
+        right_half = me >= n // 2
+
+        @pl.when((me < n - 1) & (jnp.logical_not(right_half) if inward else right_half))
         def _():
             to_right(h, 0).start()
 
-        @pl.when(me > 0)
+        @pl.when((me > 0) & (right_half if inward else jnp.logical_not(right_half)))
         def _():
             to_left(h, 0).start()
 
@@ -124,9 +126,6 @@
             def _():
                 to_left(h, k).start()
 
-    def take_far(h):
-        take(h, n - 1)
-
     def out_copy(h, piece, t):
         first = pl.multiple_of(h * width + piece * piece_width, HD)
         index = (h * pieces + piece) * tps
@@ -147,9 +146,10 @@
             device_id={"pp": last_pp, "tp": t}, device_id_type=MESH,
         )
 
-    send_own(0)
+    send_own(0, False)
+    send_own(0, True)
     if kv_heads > 1:
-        send_own(1)
+        send_own(1, False)
 
     spans = rows // SPAN
     row_in = lax.broadcasted_iota(jnp.int32, (SPAN, SPAN), 0)
@@ -165,8 +165,11 @@
 
         lax.fori_loop(0, n * spans, mask_span, 0)
 
-    low = jnp.where(me < n // 2, 0, 1)
-    far = jnp.where(me < n // 2, n - 1, 0)
+    near_count = n - 2
+    left_half = me < n // 2
+    near_slot = jnp.where(left_half, 0, 2)
+    late_slot = jnp.where(left_half, n - 2, 1)
+    last_slot = jnp.where(left_half, n - 1, 0)
     inner = (me > 0) & (me < n - 1)
 
     def block(h, slot, count, which):
@@ -215,61 +218,103 @@
 
         lax.fori_loop(0, group // 2, pair, 0)
 
-    def whole_head(h):
+    taken = set()
+
+    def need(h, furthest):
+        for k in range(1, furthest + 1):
+            if ("inner", h, k) not in taken:
+                take(h, k)
+            elif ("ends", h, k) not in taken:
+                @pl.when(jnp.logical_not(inner))
+                def _():
+                    take(h, k)
+            taken.update({("inner", h, k), ("ends", h, k)})
+
+    def relays(h, furthest, step):
+        wanted = [k for k in range(1, furthest + 1) if ("inner", h, k) not in taken]
+        taken.update(("inner", h, k) for k in wanted)
+        return [(h, k, step) for k in wanted]
+
+    def pass_on(i, steps):
+        for h, k, step in steps:
+            @pl.when((i == step) & inner)
+            def _():
+                take(h, k)
+
+    def whole_head(h, steps):
         def done(g, score):
             top = jnp.max(score, axis=1, keepdims=True)
             finish(h, g, *weigh(h, score, top, 0, n))
 
         def between(i):
             send_piece(h, i)
-            for k in range(1, n - 1):
-                @pl.when((i == min(k - 1, group // 2 - 1)) & inner)
-                def _():
-                    take(h + 1, k)
+            pass_on(i, steps)
 
         pairs(h, 0, n, done, between)
 
-    def last_head(h):
+    def first_part(h, state, slot, count, steps):
         def done(g, score):
             top = jnp.max(score, axis=1, keepdims=True)
-            mixed, total = weigh(h, score, top, low, n - 1)
-            part_mixed[g] = mixed
-            part_top[g] = jnp.broadcast_to(top, (rows, HD))
-            part_total[g] = jnp.broadcast_to(total, (rows, HD))
-
-        pairs(h, low, n - 1, done, lambda i: None)
-        take_far(h)
-
+            mixed, total = weigh(h, score, top, slot, count)
+            part_mixed[state, g] = mixed
+            part_top[state, g] = jnp.broadcast_to(top, (rows, HD))
+            part_total[state, g] = jnp.broadcast_to(total, (rows, HD))
+
+        pairs(h, slot, count, done, lambda i: pass_on(i, steps))
+
+    def add_slot(h, state, slot, final):
         def pair(i, _):
             for g in (2 * i, 2 * i + 1):
-                score = masked(score_of(h, g, far, 1), far, 1)
-                before = part_top[g]
+                score = masked(score_of(h, g, slot, 1), slot, 1)
+                before = part_top[state, g]
                 top = jnp.maximum(before, jnp.max(score, axis=1, keepdims=True))
                 fade = jnp.exp2((before - top) * LOG_SCALE)
-                mixed, total = weigh(h, score, top[:, :1], far, 1)
-                finish(h, g, part_mixed[g] * fade + mixed, part_total[g] * fade + total)
-            send_piece(h, i)
+                mixed, total = weigh(h, score, top[:, :1], slot, 1)
+                mixed = part_mixed[state, g] * fade + mixed
+                total = part_total[state, g] * fade + total
+                if final:
+                    finish(h, g, mixed, total)
+                else:
+                    part_mixed[state, g] = mixed
+                    part_top[state, g] = top
+                    part_total[state, g] = total
+            if final:
+                send_piece(h, i)
             return 0
 
         lax.fori_loop(0, group // 2, pair, 0)
 
-    for h in range(kv_heads):
-        ends = jnp.logical_not(inner)
-        if h == 0:
-            ends = me >= 0
-        for k in range(1, n - 1):
-            @pl.when(ends)
-            def _():
-                take(h, k)
-
-            if k == 1 and h + 2 < kv_heads:
-                send_own(h + 2)
+    last = kv_heads - 1
+    own_sent = 2
+    need(0, 1)
+    if kv_heads > 1:
+        send_own(1, True)
+    for h in range(max(kv_heads - 2, 0)):
+        need(h, 1)
+        if own_sent < kv_heads:
+            send_own(own_sent, False)
+            send_own(own_sent, True)
+            own_sent += 1
+        need(h, n - 1)
         q_copies[h].wait()
-        if h < kv_heads - 1:
-            take_far(h)
-            whole_head(h)
-        else:
-            last_head(h)
+        steps = relays(h + 1, n - 2, 0)
+        if h == kv_heads - 3:
+            steps += relays(last, 1, 2)
+        whole_head(h, steps)
+    need(last, n - 3)
+    q_copies[last].wait()
+    first_part(last, 1, near_slot, near_count, relays(last, n - 2, 2))
+    if kv_heads > 1:
+        wide = jnp.where(left_half, 0, 1)
+        need(last - 1, n - 2)
+        q_copies[last - 1].wait()
+        first_part(last - 1, 0, wide, n - 1, [])
+        need(last - 1, n - 1)
+        add_slot(last - 1, 0, last_slot, True)
+    need(last, n - 2)
+    add_slot(last, 1, late_slot, False)
+    need(last, n - 1)
+    add_slot(last, 1, last_slot, True)
 
     for h in range(kv_heads):
         for k in range(n - 1):
@@ -289,10 +334,6 @@
             return 0
 
         lax.fori_loop(0, pieces, drain, 0)
-
-
-def place(x_ref, o_ref):
-    o_ref[...] = x_ref[...]
 
 
 def shards(queries, keys, values, span_order):
@@ -305,14 +346,14 @@
     dma = pltpu.SemaphoreType.DMA
     result = pl.pallas_call(
         functools.partial(kernel, n, tps, pps, kv_heads, group),
-        out_shape=jax.ShapeDtypeStruct((rows // tps, tps * query_rows.shape[1]), jnp.bfloat16),
+        out_shape=pltpu.VMEM((rows // tps, tps * query_rows.shape[1]), jnp.bfloat16),
         in_specs=[
             pl.BlockSpec(memory_space=pltpu.SMEM),
             pl.BlockSpec(memory_space=pl.ANY),
             pl.BlockSpec(memory_space=pl.ANY),
             pl.BlockSpec(memory_space=pl.ANY),
         ],
-        out_specs=pl.BlockSpec(memory_space=pl.ANY),
+        out_specs=pl.BlockSpec(memory_space=pltpu.VMEM),
         scratch_shapes=[
             pltpu.VMEM(query_rows.shape, jnp.bfloat16),
             pltpu.VMEM((kv_heads, n, 2, rows, HD), jnp.bfloat16),
@@ -320,9 +361,9 @@
             pltpu.VMEM((n * rows // SPAN, rows, SPAN), jnp.float32),
             pltpu.VMEM((rows, n * rows), jnp.float32),
             pltpu.VMEM((rows, n * rows), jnp.float32),
-            pltpu.VMEM((group, rows, HD), jnp.float32),
-            pltpu.VMEM((group, rows, HD), jnp.float32),
-            pltpu.VMEM((group, rows, HD), jnp.float32),
+            pltpu.VMEM((2, group, rows, HD), jnp.float32),
+            pltpu.VMEM((2, group, rows, HD), jnp.float32),
+            pltpu.VMEM((2, group, rows, HD), jnp.float32),
             dma((kv_heads,)),
             dma((kv_heads, 2)),
             dma((kv_heads, n)),
@@ -336,16 +377,7 @@
             collective_id=0, has_side_effects=True, vmem_limit_bytes=56 * 1024 * 1024
         ),
     )(span_order, query_rows, key_local, value_local)
-    columns = result.shape[1] // 8
-    spec = pl.BlockSpec((result.shape[0], columns), lambda i: (0, i))
-    placed = pl.pallas_call(
-        place,
-        grid=(8,),
-        out_shape=jax.ShapeDtypeStruct(result.shape, result.dtype),
-        in_specs=[spec],
-        out_specs=spec,
-    )(result)
-    return placed[None]
+    return result[None]
 
 
 def solution(mesh):

time: 57.4 us -> 59.3 us (1.033)
  the two profiles are of different devices: /device:TPU:1 before, /device:TPU:9 now
where the time goes in v3:
time: 59.3 us; the launch traced here: 59.1 us
  Pallas kernels  57.8 us (97%)
  local copies, waits for them, and re-layouts  1.32 us (2%)
    pallas_call x1, Pallas kernels, shards(): pl.pallas_call(functools.partial(kernel, n, tps, pps, kv_heads, group), o...  57.8 us
    unnamed x1, local copies, waits for them, and re-layouts  1.32 us

profile of v3, /device:TPU:9, one launch (start us, length us, event | category | flops | bytes accessed | tf_op | source)
XLA Modules:
  0.0 59.1 jit_solution(1906427171893923969)
XLA Ops:
  0.0 57.8 %shard_map.46 = bf16[128,8192]{1,0:T(8,128)(2,1)S(1)} custom-call(s32[8]{0:T(128)} %order_ref.1, bf16[256,4096]{1,0:T(8,128)(2,1)} %bitcast.5, bf16[256,512]{1,0:T(8,128)(2,1)} %bitcast.6, bf16[256,512]{1,0:T(8,128)(2,1)} %bitcast.7), custom_call_target="tpu_custom_call" | custom-call | tf_op jit(solution)/shard_map/pallas_call | solution.py:347
  57.8 1.3 %copy.6 = bf16[1,128,8192]{2,1,0:T(8,128)(2,1)} copy(bf16[1,128,8192]{2,1,0:T(8,128)(2,1)S(1)} %bitcast.4) | data formatting | bytes 4194304

commit v4 on v3

--- a/solution.py
+++ b/solution.py
@@ -168,8 +168,7 @@
     near_count = n - 2
     left_half = me < n // 2
     near_slot = jnp.where(left_half, 0, 2)
-    late_slot = jnp.where(left_half, n - 2, 1)
-    last_slot = jnp.where(left_half, n - 1, 0)
+    late_slot = jnp.where(left_half, n - 2, 0)
     inner = (me > 0) & (me < n - 1)
 
     def block(h, slot, count, which):
@@ -233,7 +232,7 @@
     def relays(h, furthest, step):
         wanted = [k for k in range(1, furthest + 1) if ("inner", h, k) not in taken]
         taken.update(("inner", h, k) for k in wanted)
-        return [(h, k, step) for k in wanted]
+        return [(h, k, min(step + 2 * (k - 1), group // 2 - 1)) for k in wanted]
 
     def pass_on(i, steps):
         for h, k, step in steps:
@@ -252,37 +251,33 @@
 
         pairs(h, 0, n, done, between)
 
-    def first_part(h, state, slot, count, steps):
+    def first_part(h, slot, count, steps):
         def done(g, score):
             top = jnp.max(score, axis=1, keepdims=True)
             mixed, total = weigh(h, score, top, slot, count)
-            part_mixed[state, g] = mixed
-            part_top[state, g] = jnp.broadcast_to(top, (rows, HD))
-            part_total[state, g] = jnp.broadcast_to(total, (rows, HD))
+            part_mixed[g] = mixed
+            part_top[g] = jnp.broadcast_to(top, (rows, HD))
+            part_total[g] = jnp.broadcast_to(total, (rows, HD))
 
         pairs(h, slot, count, done, lambda i: pass_on(i, steps))
 
-    def add_slot(h, state, slot, final):
-        def pair(i, _):
-            for g in (2 * i, 2 * i + 1):
-                score = masked(score_of(h, g, slot, 1), slot, 1)
-                before = part_top[state, g]
+    def last_part(h, slot, count):
+        together = 4
+
+        def some(i, _):
+            for step in range(together):
+                g = together * i + step
+                score = masked(score_of(h, g, slot, count), slot, count)
+                before = part_top[g]
                 top = jnp.maximum(before, jnp.max(score, axis=1, keepdims=True))
                 fade = jnp.exp2((before - top) * LOG_SCALE)
-                mixed, total = weigh(h, score, top[:, :1], slot, 1)
-                mixed = part_mixed[state, g] * fade + mixed
-                total = part_total[state, g] * fade + total
-                if final:
-                    finish(h, g, mixed, total)
-                else:
-                    part_mixed[state, g] = mixed
-                    part_top[state, g] = top
-                    part_total[state, g] = total
-            if final:
-                send_piece(h, i)
+                mixed, total = weigh(h, score, top[:, :1], slot, count)
+                finish(h, g, part_mixed[g] * fade + mixed, part_total[g] * fade + total)
+                if step % 2 == 1:
+                    send_piece(h, (together * i + step) // 2)
             return 0
 
-        lax.fori_loop(0, group // 2, pair, 0)
+        lax.fori_loop(0, group // together, some, 0)
 
     last = kv_heads - 1
     own_sent = 2
@@ -299,22 +294,17 @@
         q_copies[h].wait()
         steps = relays(h + 1, n - 2, 0)
         if h == kv_heads - 3:
-            steps += relays(last, 1, 2)
+            steps += relays(last, 1, 3)
         whole_head(h, steps)
     need(last, n - 3)
     q_copies[last].wait()
-    first_part(last, 1, near_slot, near_count, relays(last, n - 2, 2))
+    first_part(last, near_slot, near_count, relays(last, n - 2, 0))
     if kv_heads > 1:
-        wide = jnp.where(left_half, 0, 1)
-        need(last - 1, n - 2)
+        need(last - 1, n - 1)
         q_copies[last - 1].wait()
-        first_part(last - 1, 0, wide, n - 1, [])
-        need(last - 1, n - 1)
-        add_slot(last - 1, 0, last_slot, True)
-    need(last, n - 2)
-    add_slot(last, 1, late_slot, False)
+        whole_head(last - 1, [])
     need(last, n - 1)
-    add_slot(last, 1, last_slot, True)
+    last_part(last, late_slot, 2)
 
     for h in range(kv_heads):
         for k in range(n - 1):
@@ -361,9 +351,9 @@
             pltpu.VMEM((n * rows // SPAN, rows, SPAN), jnp.float32),
             pltpu.VMEM((rows, n * rows), jnp.float32),
             pltpu.VMEM((rows, n * rows), jnp.float32),
-            pltpu.VMEM((2, group, rows, HD), jnp.float32),
-            pltpu.VMEM((2, group, rows, HD), jnp.float32),
-            pltpu.VMEM((2, group, rows, HD), jnp.float32),
+            pltpu.VMEM((group, rows, HD), jnp.float32),
+            pltpu.VMEM((group, rows, HD), jnp.float32),
+            pltpu.VMEM((group, rows, HD), jnp.float32),
             dma((kv_heads,)),
             dma((kv_heads, 2)),
             dma((kv_heads, n)),

time: 59.3 us -> 52.6 us (0.89)
  the two profiles are of different devices: /device:TPU:9 before, /device:TPU:1 now
where the time goes in v4:
time: 52.6 us; the launch traced here: 52.5 us
  Pallas kernels  51.1 us (97%)
  local copies, waits for them, and re-layouts  1.32 us (3%)
    pallas_call x1, Pallas kernels, shards(): pl.pallas_call(functools.partial(kernel, n, tps, pps, kv_heads, group), o...  51.1 us
    unnamed x1, local copies, waits for them, and re-layouts  1.32 us

profile of v4, /device:TPU:1, one launch (start us, length us, event | category | flops | bytes accessed | tf_op | source)
XLA Modules:
  0.0 52.5 jit_solution(3533010648968089995)
XLA Ops:
  0.0 51.1 %shard_map.46 = bf16[128,8192]{1,0:T(8,128)(2,1)S(1)} custom-call(s32[8]{0:T(128)} %order_ref.1, bf16[256,4096]{1,0:T(8,128)(2,1)} %bitcast.5, bf16[256,512]{1,0:T(8,128)(2,1)} %bitcast.6, bf16[256,512]{1,0:T(8,128)(2,1)} %bitcast.7), custom_call_target="tpu_custom_call" | custom-call | tf_op jit(solution)/shard_map/pallas_call | solution.py:337
  51.1 1.3 %copy.6 = bf16[1,128,8192]{2,1,0:T(8,128)(2,1)} copy(bf16[1,128,8192]{2,1,0:T(8,128)(2,1)S(1)} %bitcast.4) | data formatting | bytes 4194304
